TPU v7x, 32 devices: a whole 2x2x4 slice. The times are simulated.
32 devices in a mesh: section: 4 (over y, x), expert: 8 (over z, core).
Axes of the slice: x: 2, y: 2, z: 4, core: 2. Of those that a mesh axis runs over, the one named last changes fastest.
Arguments:
- forward_input: bfloat16 [4, 576, 4096], P('section', 'expert'), may hold values from -6 to 6
- backward_cotangent: bfloat16 [4, 576, 4096], P('section', 'expert'), may hold values from -6 to 6
- saved_input: bfloat16 [4, 576, 4096], P('section', 'expert'), may hold values from -6 to 6
- saved_hidden: bfloat16 [4, 8, 360, 1536], P('section', 'expert'), may hold values from -8 to 8
- norm_gain: float32 [4, 4096], P('section'), may hold values from 0.5 to 2
- forward_experts: int32 [4, 576, 4], P('section', 'expert'), may hold values from 0 to 7, all different within a row; in each aligned block of 72 rows (0 to 71, 72 to 143, ..., all dimensions but the last counted through in order) at most 45 rows name the same one
- forward_gates: float32 [4, 576, 4], P('section', 'expert'), may hold values from 0.05 to 1
- backward_experts: int32 [4, 576, 4], P('section', 'expert'), may hold values from 0 to 7, all different within a row; in each aligned block of 72 rows (0 to 71, 72 to 143, ..., all dimensions but the last counted through in order) at most 45 rows name the same one
- backward_gates: float32 [4, 576, 4], P('section', 'expert'), may hold values from 0.05 to 1
- gate_up_weight: bfloat16 [4, 8, 4096, 1536], P('section', 'expert'), may hold values from -0.09375 to 0.09375
- down_weight: bfloat16 [4, 8, 768, 4096], P('section', 'expert'), may hold values from -0.21875 to 0.21875
Outputs:
- forward_output: bfloat16 [4, 576, 4096], P('section', 'expert')
- input_gradient: bfloat16 [4, 576, 4096], P('section', 'expert')
Inputs may be any that keep to these rules, and one draw needn't show every extreme that they name: `forward_experts`: each token names 4 distinct experts. In the rows of one device (aligned blocks of 72 tokens) no expert is named by more than 45 entries, and in some device's rows some expert is named by exactly 45. `backward_experts`: same law as forward_experts, drawn independently.
All inputs are finite; a program needn't handle non-finite values.
Results may differ from a plain program's by a relative error of at most 0.0054.
Values may be sent and summed in bfloat16 or wider, within the bound.
A program may use at most 128 MiB of HBM per device.

v0:
```python
import jax
import jax.numpy as jnp
from jax import lax
from jax.sharding import PartitionSpec as P

EPSILON = 1e-06


def passed_along(value, axis, steps):
    count = lax.axis_size(axis)
    initial, last = (max(0, -steps), min(count, count - steps))
    return lax.ppermute(value, axis, [(source, source + steps) for source in range(initial, last)])


def norm_scale(values, gain_row):
    widened = values.astype(jnp.float32)
    inverse = lax.rsqrt(jnp.mean(widened * widened, axis=-1, keepdims=True) + EPSILON)
    return widened * inverse * gain_row


def dense_weights(expert_ids, gates, expert_count):
    weights = gates / jnp.sum(gates, axis=-1, keepdims=True)
    onehot = expert_ids[:, :, None] == jnp.arange(expert_count, dtype=jnp.int32)[None, None, :]
    return jnp.sum(jnp.where(onehot, weights[:, :, None], 0.0), axis=1)


def local(
    forward_input,
    backward_cotangent,
    saved_input,
    saved_hidden,
    norm_gain,
    forward_experts,
    forward_gates,
    backward_experts,
    backward_gates,
    gate_up_weight,
    down_weight,
):
    peer_count = lax.axis_size("expert")
    me = lax.axis_index("expert")
    table = jnp.concatenate(
        [
            dense_weights(forward_experts[0], forward_gates[0], peer_count),
            dense_weights(backward_experts[0], backward_gates[0], peer_count),
        ],
        axis=1,
    )
    tables = lax.all_gather(table, "expert", axis=0, tiled=True)
    weight_f = lax.dynamic_slice_in_dim(tables, me, 1, axis=1)
    weight_b = lax.dynamic_slice_in_dim(tables, peer_count + me, 1, axis=1)
    moved_input, moved_cotangent = passed_along((forward_input, backward_cotangent), "section", 1)
    is_first = lax.axis_index("section") == 0
    layer_in = jnp.where(is_first, forward_input, moved_input)[0]
    cotangent = jnp.where(is_first, backward_cotangent, moved_cotangent)[0]
    token_count = layer_in.shape[0]
    slot_total = saved_hidden.shape[2]
    capacity = slot_total // peer_count
    gain_row = norm_gain[0]
    weight_in = gate_up_weight[0, 0]
    weight_down = down_weight[0, 0]
    hidden_width = weight_down.shape[0]
    normed = norm_scale(layer_in, gain_row).astype(jnp.bfloat16)
    all_normed = lax.all_gather(normed, "expert", axis=0, tiled=True)
    all_cotangent = lax.all_gather(cotangent, "expert", axis=0, tiled=True)
    projected = jnp.dot(all_normed, weight_in, preferred_element_type=jnp.float32)
    hidden = (jax.nn.silu(projected[:, :hidden_width]) * projected[:, hidden_width:]).astype(
        jnp.bfloat16
    )
    served = jnp.dot(hidden, weight_down, preferred_element_type=jnp.float32)
    served = (served * weight_f).astype(jnp.bfloat16)
    mixture = lax.psum_scatter(served, "expert", scatter_dimension=0, tiled=True)
    forward_output = (layer_in.astype(jnp.float32) + mixture.astype(jnp.float32)).astype(
        jnp.bfloat16
    )
    routed = (weight_b > 0.0).reshape(peer_count, token_count)
    slot = jnp.cumsum(routed.astype(jnp.int32), axis=1) - 1
    spread = (
        (slot[:, :, None] == jnp.arange(capacity, dtype=jnp.int32)[None, None, :])
        & routed[:, :, None]
    ).astype(jnp.bfloat16)
    saved = jnp.einsum(
        "jts,jsf->jtf",
        spread,
        saved_hidden[0, 0].reshape(peer_count, capacity, -1),
        preferred_element_type=jnp.float32,
    ).reshape(peer_count * token_count, -1)
    scaled = (weight_b * all_cotangent.astype(jnp.float32)).astype(jnp.bfloat16)
    grad_hidden = lax.dot_general(
        scaled, weight_down, (((1,), (1,)), ((), ())), preferred_element_type=jnp.float32
    )
    gate, up = (saved[:, :hidden_width], saved[:, hidden_width:])
    sig = jax.nn.sigmoid(gate)
    grad_both = jnp.concatenate(
        [grad_hidden * up * sig * (1.0 + gate * (1.0 - sig)), grad_hidden * gate * sig], axis=1
    ).astype(jnp.bfloat16)
    grads = lax.dot_general(
        grad_both, weight_in, (((1,), (1,)), ((), ())), preferred_element_type=jnp.float32
    ).astype(jnp.bfloat16)
    grad_normed = lax.psum_scatter(grads, "expert", scatter_dimension=0, tiled=True).astype(
        jnp.float32
    )

    def apply_norm(inputs):
        return norm_scale(inputs, gain_row)

    primal, pullback = jax.vjp(apply_norm, saved_input[0].astype(jnp.float32))
    input_gradient = (cotangent.astype(jnp.float32) + pullback(grad_normed)[0]).astype(jnp.bfloat16)
    return (forward_output[None], input_gradient[None])


def solution(mesh):
    row = P("section", "expert", None)
    block = P("section", "expert", None, None)
    in_specs = (row, row, row, block, P("section", None), row, row, row, row, block, block)
    return jax.shard_map(local, mesh=mesh, in_specs=in_specs, out_specs=(row, row), check_vma=False)
```

profile of v0, /device:TPU:0, one launch (start us, length us, event | category | flops | bytes accessed | tf_op | source)
XLA Modules:
  0.0 298.4 jit_solution(10791374151857974960)
XLA Ops:
  7.3 5.0 %collective-permute-start.1 = (bf16[1,72,4096]{2,1,0:T(8,128)(2,1)}, bf16[1,72,4096]{2,1,0:T(8,128)(2,1)S(1)}, u32[]{:S(2)}, u32[]{:S(2)}) collective-permute-start(bf16[1,72,4096]{2,1,0:T(8,128)(2,1)} %param.12), channel_id=1, source_target_pairs={{0,8},{8,16},{16,24},{1,9},{9,17},{17,25},{2,10},{10,18},{18,26},{... | collective-permute-start | bytes 1769480 | tf_op jit(solution)/shard_map/ppermute | solution.py:12
  12.3 12.8 %collective-permute-done.1 = bf16[1,72,4096]{2,1,0:T(8,128)(2,1)S(1)} collective-permute-done((bf16[1,72,4096]{2,1,0:T(8,128)(2,1)}, bf16[1,72,4096]{2,1,0:T(8,128)(2,1)S(1)}, u32[]{:S(2)}, u32[]{:S(2)}) %collective-permute-start.1) | collective-permute-done | bytes 589856 | tf_op jit(solution)/shard_map/ppermute | solution.py:12
  25.1 2.0 broadcast_select_fusion
  27.3 14.3 %all-gather.1 = f32[8,72,16]{1,2,0:T(8,128)S(1)} all-gather(f32[1,72,16]{1,2,0:T(8,128)S(1)} %maximum_bitcast_fusion), channel_id=1, replica_groups=mesh['section'=4,'expert'=8] {'expert'}, dimensions={0}, use_global_device_ids=true | all-gather | bytes 41472 | tf_op jit(solution)/shard_map/all_gather | solution.py:49
  41.7 0.3 reshape_squeeze.3
  42.1 0.1 reshape.92
  42.2 0.2 reduce_window_sum.11
  42.5 2.4 fusion.34
  44.9 35.2 %all-gather.7.cloned.1.call-done = bf16[1,576,4096]{2,1,0:T(8,128)(2,1)} async-done(((bf16[1,72,4096]{2,1,0:T(8,128)(2,1)}), bf16[1,576,4096]{2,1,0:T(8,128)(2,1)}) %all-gather.7.cloned.1.call-update) | async-done | bytes 4718608 | tf_op jit(solution)/shard_map/all_gather | solution.py:65
  80.1 9.4 %fusion.16 = (bf16[576,768]{1,0:T(8,128)(2,1)S(1)}, bf16[576,768]{1,0:T(8,128)(2,1)S(1)}) fusion(f32[576,1536]{1,0:T(8,128)} %bitcast.55, bf16[1,1,768,4096]{3,2,1,0:T(8,128)(2,1)} %param.21, bf16[1,576,4096]{2,1,0:T(8,128)(2,1)} %all-gather.7.cloned.1.call-done, f32[576]{0:T(1024)S(1)} %get-tuple-element.4), kind=kOutput, calls=%fused_computation.16 | convolution fusion | flops 3636707328 | bytes 16320768 | tf_op jit(solution)/shard_map/dot_general | solution.py:89
  89.6 18.4 %fusion.8 = bf16[576,4096]{1,0:T(8,128)(2,1)} fusion(bf16[1,1,4096,1536]{3,2,1,0:T(8,128)(2,1)} %param.20, bf16[576,768]{1,0:T(8,128)(2,1)S(1)} %get-tuple-element.9, bf16[576,768]{1,0:T(8,128)(2,1)S(1)} %get-tuple-element.8), kind=kOutput, calls=%fused_computation.10 | convolution fusion | flops 7253655552 | bytes 19070976 | tf_op jit(solution)/shard_map/dot_general | solution.py:97
  108.0 1.0 copy-done.3
  109.0 3.4 %collective-permute-start = (bf16[1,72,4096]{2,1,0:T(8,128)(2,1)S(1)}, bf16[1,72,4096]{2,1,0:T(8,128)(2,1)S(1)}, u32[]{:S(2)}, u32[]{:S(2)}) collective-permute-start(bf16[1,72,4096]{2,1,0:T(8,128)(2,1)S(1)} %copy-done.3), channel_id=1, source_target_pairs={{0,8},{8,16},{16,24},{1,9},{9,17},{17,25},{2,10},{10,18},{18,26},{... | collective-permute-start | bytes 1769480 | tf_op jit(solution)/shard_map/ppermute | solution.py:12
  112.4 12.9 %collective-permute-done = bf16[1,72,4096]{2,1,0:T(8,128)(2,1)S(1)} collective-permute-done((bf16[1,72,4096]{2,1,0:T(8,128)(2,1)S(1)}, bf16[1,72,4096]{2,1,0:T(8,128)(2,1)S(1)}, u32[]{:S(2)}, u32[]{:S(2)}) %collective-permute-start) | collective-permute-done | bytes 589856 | tf_op jit(solution)/shard_map/ppermute | solution.py:12
  125.3 0.3 fusion.23
  125.6 36.1 %reduce-scatter.5.cloned.1.call-done = bf16[72,4096]{1,0:T(8,128)(2,1)} async-done(((bf16[576,4096]{1,0:T(8,128)(2,1)}), bf16[72,4096]{1,0:T(8,128)(2,1)}) %reduce-scatter.5.cloned.1.call-update) | async-done | bytes 589840 | tf_op jit(solution)/shard_map/reduce_scatter | solution.py:100
  161.7 1.4 fusion.27
  163.2 2.6 fusion.32
  165.9 0.2 reduce-scatter.3.cloned.1.call-start
  166.1 50.0 %all-gather.5.cloned.1.call-done = bf16[576,4096]{1,0:T(8,128)(2,1)} async-done(((bf16[72,4096]{1,0:T(8,128)(2,1)}), bf16[576,4096]{1,0:T(8,128)(2,1)}) %all-gather.5.cloned.1.call-update) | async-done | bytes 4718608 | tf_op jit(solution)/shard_map/all_gather | solution.py:64
  216.1 11.5 %fusion.2 = f32[576,1536]{1,0:T(8,128)S(1)} fusion(bf16[576,4096]{1,0:T(8,128)(2,1)} %all-gather.5.cloned.1.call-done, bf16[1,1,4096,1536]{3,2,1,0:T(8,128)(2,1)} %param.20), kind=kOutput, calls=%fused_computation.2 | convolution fusion | flops 7247757312 | bytes 20840448 | tf_op jit(solution)/shard_map/dot_general | solution.py:66
  227.5 8.4 %multiply_convert_fusion = bf16[576,4096]{1,0:T(8,128)(2,1)} fusion(bf16[1,1,768,4096]{3,2,1,0:T(8,128)(2,1)} %param.21, f32[576]{0:T(1024)S(1)} %get-tuple-element.5, f32[576,1536]{1,0:T(8,128)S(1)} %fusion.2), kind=kOutput, calls=%fused_computation.6 | convolution fusion | flops 3631251456 | bytes 14551296 | tf_op jit(solution)/shard_map/dot_general | solution.py:70
  235.9 53.9 %reduce-scatter.3.cloned.1.call-done = bf16[72,4096]{1,0:T(8,128)(2,1)} async-done(((bf16[576,4096]{1,0:T(8,128)(2,1)}), bf16[72,4096]{1,0:T(8,128)(2,1)}) %reduce-scatter.3.cloned.1.call-update) | async-done | bytes 589840 | tf_op jit(solution)/shard_map/reduce_scatter | solution.py:72
  289.9 2.0 fusion.31
  (38 shorter events, 0.5 us)
Async XLA Ops:
  7.2 20.0 %copy-start.5 = (f32[1,72,4]{1,2,0:T(4,128)S(1)}, f32[1,72,4]{1,2,0:T(4,128)}, u32[]{:S(2)}) copy-start(f32[1,72,4]{1,2,0:T(4,128)} %param.19) | copy-start | bytes 3460
  7.2 20.0 %copy-start.6 = (f32[1,72,4]{1,2,0:T(4,128)S(1)}, f32[1,72,4]{1,2,0:T(4,128)}, u32[]{:S(2)}) copy-start(f32[1,72,4]{1,2,0:T(4,128)} %param.17) | copy-start | bytes 3460
  7.2 20.1 %copy-start.7 = (s32[1,72,4]{1,2,0:T(4,128)S(1)}, s32[1,72,4]{1,2,0:T(4,128)}, u32[]{:S(2)}) copy-start(s32[1,72,4]{1,2,0:T(4,128)} %param.18) | copy-start | bytes 3460
  7.2 20.1 %copy-start.8 = (s32[1,72,4]{1,2,0:T(4,128)S(1)}, s32[1,72,4]{1,2,0:T(4,128)}, u32[]{:S(2)}) copy-start(s32[1,72,4]{1,2,0:T(4,128)} %param.16) | copy-start | bytes 3460
  7.2 34.5 %copy-start.2 = (bf16[1,1,360,1536]{3,2,1,0:T(8,128)(2,1)S(1)}, bf16[1,1,360,1536]{3,2,1,0:T(8,128)(2,1)}, u32[]{:S(2)}) copy-start(bf16[1,1,360,1536]{3,2,1,0:T(8,128)(2,1)} %param.14) | copy-start | bytes 3317764
  7.2 72.9 %all-gather.7.cloned.1.call-start = ((), (), s32[]{:S(2)}) async-start(), calls=%async_computation.5 | async-start | bytes 5308416 | tf_op jit(solution)/shard_map/all_gather | solution.py:65
  7.3 17.9 %collective-permute-start.1 = (bf16[1,72,4096]{2,1,0:T(8,128)(2,1)}, bf16[1,72,4096]{2,1,0:T(8,128)(2,1)S(1)}, u32[]{:S(2)}, u32[]{:S(2)}) collective-permute-start(bf16[1,72,4096]{2,1,0:T(8,128)(2,1)} %param.12), channel_id=1, source_target_pairs={{0,8},{8,16},{16,24},{1,9},{9,17},{17,25},{2,10},{10,18},{18,26},{... | collective-permute-start | bytes 1769480 | tf_op jit(solution)/shard_map/ppermute | solution.py:12
  27.1 134.6 %reduce-scatter.5.cloned.1.call-start = ((), (), s32[]{:S(2)}) async-start(), calls=%async_computation.4 | async-start | bytes 5308416 | tf_op jit(solution)/shard_map/reduce_scatter | solution.py:100
  107.9 1.1 copy-start.3
  107.9 53.8 %copy-start.1 = (bf16[1,72,4096]{2,1,0:T(8,128)(2,1)S(1)}, bf16[1,72,4096]{2,1,0:T(8,128)(2,1)}, u32[]{:S(2)}) copy-start(bf16[1,72,4096]{2,1,0:T(8,128)(2,1)} %param.13) | copy-start | bytes 1769476
  107.9 53.8 %copy-start.4 = (f32[1,4096]{1,0:T(1,128)S(1)}, f32[1,4096]{1,0:T(1,128)}, u32[]{:S(2)}) copy-start(f32[1,4096]{1,0:T(1,128)} %param.15) | copy-start | bytes 49156
  108.0 55.2 %copy-start = (bf16[1,72,4096]{2,1,0:T(8,128)(2,1)S(1)}, bf16[1,72,4096]{2,1,0:T(8,128)(2,1)}, u32[]{:S(2)}) copy-start(bf16[1,72,4096]{2,1,0:T(8,128)(2,1)} %broadcast_select_fusion) | copy-start | bytes 1769476
  108.0 108.1 %all-gather.5.cloned.1.call-start = ((), (), s32[]{:S(2)}) async-start(), calls=%async_computation.2 | async-start | bytes 5308416 | tf_op jit(solution)/shard_map/all_gather | solution.py:64
  109.0 16.3 %collective-permute-start = (bf16[1,72,4096]{2,1,0:T(8,128)(2,1)S(1)}, bf16[1,72,4096]{2,1,0:T(8,128)(2,1)S(1)}, u32[]{:S(2)}, u32[]{:S(2)}) collective-permute-start(bf16[1,72,4096]{2,1,0:T(8,128)(2,1)S(1)} %copy-done.3), channel_id=1, source_target_pairs={{0,8},{8,16},{16,24},{1,9},{9,17},{17,25},{2,10},{10,18},{18,26},{... | collective-permute-start | bytes 1769480 | tf_op jit(solution)/shard_map/ppermute | solution.py:12
  165.9 124.0 %reduce-scatter.3.cloned.1.call-start = ((), (), s32[]{:S(2)}) async-start(), calls=%async_computation.3 | async-start | bytes 5308416 | tf_op jit(solution)/shard_map/reduce_scatter | solution.py:72
Sparse Core Ops, SparseCore 0:
  27.2 52.8 all-gather.6
  108.1 53.6 reduce-scatter.4
  166.0 50.0 all-gather.4
  236.1 53.7 reduce-scatter.2
where the time goes:
time: 299 us; the launch traced here: 298 us
  waiting for transfers between devices  201 us (67%)
  matrix products  50 us (17%)
  blocking collectives  14.3 us (5%)
  between operations  14 us (5%)
  starting transfers between devices  8.75 us (3%)
  other arithmetic  8.72 us (3%)
    reduce_scatter x1, waiting for transfers between devices, local(): lax.psum_scatter(served, 'expert', scatter_dimension=0, tiled=True)  53.9 us
    all_gather x1, waiting for transfers between devices, local(): all_normed = lax.all_gather(normed, 'expert', axis=0, tiled=True)  50 us
    reduce_scatter x1, waiting for transfers between devices, local(): lax.psum_scatter(grads, 'expert', scatter_dimension=0, tiled=True)  36.1 us
    all_gather x1, waiting for transfers between devices, local(): all_cotangent = lax.all_gather(cotangent, 'expert', axis=0, tiled=True)  35.2 us
    ppermute x2, waiting for transfers between devices, passed_along(): lax.ppermute(value, axis, [(source, source + steps) for source in range(i...  25.8 us
    dot_general x1, matrix products, local(): lax.dot_general(grad_both, weight_in, (((1,), (1,)), ((), ())), preferred...  18.4 us
    all_gather x1, blocking collectives, local(): tables = lax.all_gather(table, 'expert', axis=0, tiled=True)  14.3 us
    dot_general x1, matrix products, local(): jnp.dot(all_normed, weight_in, preferred_element_type=jnp.float32)  11.5 us
  transfers between devices with their start and end apart: 6, of which 6 were waited for; matrix products, arithmetic and copies ran while one was open for 1% of the time, Pallas kernels for 0%

commit v1 on v0

--- a/solution.py
+++ b/solution.py
@@ -61,8 +61,11 @@
     weight_down = down_weight[0, 0]
     hidden_width = weight_down.shape[0]
     normed = norm_scale(layer_in, gain_row).astype(jnp.bfloat16)
-    all_normed = lax.all_gather(normed, "expert", axis=0, tiled=True)
-    all_cotangent = lax.all_gather(cotangent, "expert", axis=0, tiled=True)
+    all_normed, all_cotangent = jnp.split(
+        lax.all_gather(jnp.concatenate([normed, cotangent], axis=1), "expert", axis=0, tiled=True),
+        [normed.shape[1]],
+        axis=1,
+    )
     projected = jnp.dot(all_normed, weight_in, preferred_element_type=jnp.float32)
     hidden = (jax.nn.silu(projected[:, :hidden_width]) * projected[:, hidden_width:]).astype(
         jnp.bfloat16

time: 299 us -> 279 us (0.933)
  waiting for transfers between devices: 201 us -> 183 us
    all_gather x2 -> x1, waiting for transfers between devices: 85.2 us -> 75.3 us  [local(): lax.all_gather(jnp.concatenate([normed, cotangent], axis=1), 'expert', ax...]
    ppermute x2, waiting for transfers between devices: 25.8 us -> 20.5 us  [passed_along(): lax.ppermute(value, axis, [(source, source + steps) for source in range(i...]
  transfers between devices with their start and end apart: 6 -> 5, of which waited for: 6 -> 5; matrix products, arithmetic and copies ran while one was open for 1% -> 9% of each run, Pallas kernels for 0% -> 0%
where the time goes in v1:
time: 279 us
  waiting for transfers between devices  183 us (66%)
  matrix products  50.2 us (18%)
  blocking collectives  14.2 us (5%)
  between operations  14 us (5%)
  starting transfers between devices  8.71 us (3%)
  other arithmetic  7.87 us (3%)
    all_gather x1, waiting for transfers between devices, local(): lax.all_gather(jnp.concatenate([normed, cotangent], axis=1), 'expert', ax...  75.3 us
    reduce_scatter x1, waiting for transfers between devices, local(): lax.psum_scatter(served, 'expert', scatter_dimension=0, tiled=True)  54.1 us
    reduce_scatter x1, waiting for transfers between devices, local(): lax.psum_scatter(grads, 'expert', scatter_dimension=0, tiled=True)  33.4 us
    ppermute x2, waiting for transfers between devices, passed_along(): lax.ppermute(value, axis, [(source, source + steps) for source in range(i...  20.5 us
    dot_general x1, matrix products, local(): lax.dot_general(grad_both, weight_in, (((1,), (1,)), ((), ())), preferred...  18.4 us
    all_gather x1, blocking collectives, local(): tables = lax.all_gather(table, 'expert', axis=0, tiled=True)  14.2 us
    dot_general x1, matrix products, local(): jnp.dot(all_normed, weight_in, preferred_element_type=jnp.float32)  11.5 us
    dot_general x1, matrix products, local(): lax.dot_general(scaled, weight_down, (((1,), (1,)), ((), ())), preferred_...  9.4 us
  transfers between devices with their start and end apart: 5, of which 5 were waited for; matrix products, arithmetic and copies ran while one was open for 9% of the time, Pallas kernels for 0%

profile of v1, /device:TPU:0, one launch (start us, length us, event | category | flops | bytes accessed | tf_op | source)
XLA Modules:
  0.0 278.9 jit_solution(14671534145485425485)
XLA Ops:
  7.2 5.0 %collective-permute-start = (bf16[1,72,4096]{2,1,0:T(8,128)(2,1)}, bf16[1,72,4096]{2,1,0:T(8,128)(2,1)S(1)}, u32[]{:S(2)}, u32[]{:S(2)}) collective-permute-start(bf16[1,72,4096]{2,1,0:T(8,128)(2,1)} %param.11), channel_id=1, source_target_pairs={{0,8},{8,16},{16,24},{1,9},{9,17},{17,25},{2,10},{10,18},{18,26},{... | collective-permute-start | bytes 1769480 | tf_op jit(solution)/shard_map/ppermute | solution.py:12
  12.2 3.4 %collective-permute-start.1 = (bf16[1,72,4096]{2,1,0:T(8,128)(2,1)}, bf16[1,72,4096]{2,1,0:T(8,128)(2,1)S(1)}, u32[]{:S(2)}, u32[]{:S(2)}) collective-permute-start(bf16[1,72,4096]{2,1,0:T(8,128)(2,1)} %param.12), channel_id=1, source_target_pairs={{0,8},{8,16},{16,24},{1,9},{9,17},{17,25},{2,10},{10,18},{18,26},{... | collective-permute-start | bytes 1769480 | tf_op jit(solution)/shard_map/ppermute | solution.py:12
  15.7 10.6 %collective-permute-done = bf16[1,72,4096]{2,1,0:T(8,128)(2,1)S(1)} collective-permute-done((bf16[1,72,4096]{2,1,0:T(8,128)(2,1)}, bf16[1,72,4096]{2,1,0:T(8,128)(2,1)S(1)}, u32[]{:S(2)}, u32[]{:S(2)}) %collective-permute-start) | collective-permute-done | bytes 589856 | tf_op jit(solution)/shard_map/ppermute | solution.py:12
  26.2 1.4 fusion.22
  27.6 0.2 fusion.24
  27.9 9.9 %collective-permute-done.1 = bf16[1,72,4096]{2,1,0:T(8,128)(2,1)S(1)} collective-permute-done((bf16[1,72,4096]{2,1,0:T(8,128)(2,1)}, bf16[1,72,4096]{2,1,0:T(8,128)(2,1)S(1)}, u32[]{:S(2)}, u32[]{:S(2)}) %collective-permute-start.1) | collective-permute-done | bytes 589856 | tf_op jit(solution)/shard_map/ppermute | solution.py:12
  37.9 1.1 pad_maximum_fusion
  39.2 14.2 %all-gather = f32[8,72,16]{1,2,0:T(8,128)S(1)} all-gather(f32[1,72,16]{1,2,0:T(8,128)S(1)} %maximum_bitcast_fusion), channel_id=1, replica_groups=mesh['section'=4,'expert'=8] {'expert'}, dimensions={0}, use_global_device_ids=true | all-gather | bytes 41472 | tf_op jit(solution)/shard_map/all_gather | solution.py:49
  53.5 0.1 reshape.97
  53.6 0.1 reshape.92
  53.7 0.2 reduce_window_sum.11
  53.9 0.3 reshape_squeeze.3
  54.3 2.5 fusion.33
  56.8 75.3 %all-gather.3.cloned.1.call-done = bf16[576,8192]{1,0:T(8,128)(2,1)} async-done(((bf16[72,8192]{1,0:T(8,128)(2,1)}), bf16[576,8192]{1,0:T(8,128)(2,1)}) %all-gather.3.cloned.1.call-update) | async-done | bytes 9437200 | tf_op jit(solution)/shard_map/all_gather | solution.py:65
  132.1 9.4 %fusion.15 = (bf16[576,768]{1,0:T(8,128)(2,1)S(1)}, bf16[576,768]{1,0:T(8,128)(2,1)S(1)}) fusion(f32[576,1536]{1,0:T(8,128)} %bitcast.45, bf16[1,1,768,4096]{3,2,1,0:T(8,128)(2,1)} %param.21, bf16[576,8192]{1,0:T(8,128)(2,1)} %all-gather.3.cloned.1.call-done, f32[576]{0:T(1024)S(1)} %get-tuple-element.4), kind=kOutput, calls=%fused_computation.16 | convolution fusion | flops 3636707328 | bytes 16320768 | tf_op jit(solution)/shard_map/dot_general | solution.py:92
  141.5 18.4 %fusion.7 = bf16[576,4096]{1,0:T(8,128)(2,1)} fusion(bf16[1,1,4096,1536]{3,2,1,0:T(8,128)(2,1)} %param.20, bf16[576,768]{1,0:T(8,128)(2,1)S(1)} %get-tuple-element.9, bf16[576,768]{1,0:T(8,128)(2,1)S(1)} %get-tuple-element.8), kind=kOutput, calls=%fused_computation.9 | convolution fusion | flops 7253655552 | bytes 19070976 | tf_op jit(solution)/shard_map/dot_general | solution.py:100
  159.9 0.2 reduce-scatter.3.cloned.1.call-start
  160.1 11.5 %fusion.2 = f32[576,1536]{1,0:T(8,128)S(1)} fusion(bf16[1,1,4096,1536]{3,2,1,0:T(8,128)(2,1)} %param.20, bf16[576,8192]{1,0:T(8,128)(2,1)} %all-gather.3.cloned.1.call-done), kind=kOutput, calls=%fused_computation.2 | convolution fusion | flops 7247757312 | bytes 20840448 | tf_op jit(solution)/shard_map/dot_general | solution.py:69
  171.6 8.5 %multiply_convert_fusion.1 = bf16[576,4096]{1,0:T(8,128)(2,1)} fusion(bf16[1,1,768,4096]{3,2,1,0:T(8,128)(2,1)} %param.21, f32[576]{0:T(1024)S(1)} %get-tuple-element.5, f32[576,1536]{1,0:T(8,128)S(1)} %fusion.2), kind=kOutput, calls=%fused_computation.5 | convolution fusion | flops 3631251456 | bytes 14551296 | tf_op jit(solution)/shard_map/dot_general | solution.py:73
  180.1 33.4 %reduce-scatter.5.cloned.1.call-done = bf16[72,4096]{1,0:T(8,128)(2,1)} async-done(((bf16[576,4096]{1,0:T(8,128)(2,1)}), bf16[72,4096]{1,0:T(8,128)(2,1)}) %reduce-scatter.5.cloned.1.call-update) | async-done | bytes 589840 | tf_op jit(solution)/shard_map/reduce_scatter | solution.py:103
  213.5 1.5 fusion.26
  215.0 54.1 %reduce-scatter.3.cloned.1.call-done = bf16[72,4096]{1,0:T(8,128)(2,1)} async-done(((bf16[576,4096]{1,0:T(8,128)(2,1)}), bf16[72,4096]{1,0:T(8,128)(2,1)}) %reduce-scatter.3.cloned.1.call-update) | async-done | bytes 589840 | tf_op jit(solution)/shard_map/reduce_scatter | solution.py:75
  269.1 2.0 fusion.30
  271.1 1.2 fusion.31
  (37 shorter events, 0.4 us)
Async XLA Ops:
  7.2 30.6 %copy-start.3 = (bf16[1,72,4096]{2,1,0:T(8,128)(2,1)S(1)}, bf16[1,72,4096]{2,1,0:T(8,128)(2,1)}, u32[]{:S(2)}) copy-start(bf16[1,72,4096]{2,1,0:T(8,128)(2,1)} %param.12) | copy-start | bytes 1769476
  7.2 20.5 %copy-start.4 = (f32[1,4096]{1,0:T(1,128)S(1)}, f32[1,4096]{1,0:T(1,128)}, u32[]{:S(2)}) copy-start(f32[1,4096]{1,0:T(1,128)} %param.15) | copy-start | bytes 49156
  7.2 124.9 %all-gather.3.cloned.1.call-start = ((), (), s32[]{:S(2)}) async-start(), calls=%async_computation.2 | async-start | bytes 10616832 | tf_op jit(solution)/shard_map/all_gather | solution.py:65
  7.2 19.0 %collective-permute-start = (bf16[1,72,4096]{2,1,0:T(8,128)(2,1)}, bf16[1,72,4096]{2,1,0:T(8,128)(2,1)S(1)}, u32[]{:S(2)}, u32[]{:S(2)}) collective-permute-start(bf16[1,72,4096]{2,1,0:T(8,128)(2,1)} %param.11), channel_id=1, source_target_pairs={{0,8},{8,16},{16,24},{1,9},{9,17},{17,25},{2,10},{10,18},{18,26},{... | collective-permute-start | bytes 1769480 | tf_op jit(solution)/shard_map/ppermute | solution.py:12
  12.2 25.5 %collective-permute-start.1 = (bf16[1,72,4096]{2,1,0:T(8,128)(2,1)}, bf16[1,72,4096]{2,1,0:T(8,128)(2,1)S(1)}, u32[]{:S(2)}, u32[]{:S(2)}) collective-permute-start(bf16[1,72,4096]{2,1,0:T(8,128)(2,1)} %param.12), channel_id=1, source_target_pairs={{0,8},{8,16},{16,24},{1,9},{9,17},{17,25},{2,10},{10,18},{18,26},{... | collective-permute-start | bytes 1769480 | tf_op jit(solution)/shard_map/ppermute | solution.py:12
  37.8 1.3 copy-start.6
  37.8 1.3 copy-start.5
  37.8 1.3 copy-start.7
  37.8 1.3 copy-start.8
  37.9 16.1 %copy-start.2 = (bf16[1,1,360,1536]{3,2,1,0:T(8,128)(2,1)S(1)}, bf16[1,1,360,1536]{3,2,1,0:T(8,128)(2,1)}, u32[]{:S(2)}) copy-start(bf16[1,1,360,1536]{3,2,1,0:T(8,128)(2,1)} %param.14) | copy-start | bytes 3317764
  39.0 174.5 %reduce-scatter.5.cloned.1.call-start = ((), (), s32[]{:S(2)}) async-start(), calls=%async_computation.4 | async-start | bytes 5308416 | tf_op jit(solution)/shard_map/reduce_scatter | solution.py:103
  159.9 109.2 %reduce-scatter.3.cloned.1.call-start = ((), (), s32[]{:S(2)}) async-start(), calls=%async_computation.3 | async-start | bytes 5308416 | tf_op jit(solution)/shard_map/reduce_scatter | solution.py:75
  180.1 33.4 %copy-start = (bf16[1,72,4096]{2,1,0:T(8,128)(2,1)S(1)}, bf16[1,72,4096]{2,1,0:T(8,128)(2,1)}, u32[]{:S(2)}) copy-start(bf16[1,72,4096]{2,1,0:T(8,128)(2,1)} %param.13) | copy-start | bytes 1769476
  213.5 57.6 %copy-start.1 = (bf16[72,4096]{1,0:T(8,128)(2,1)S(1)}, bf16[72,4096]{1,0:T(8,128)(2,1)}, u32[]{:S(2)}) copy-start(bf16[72,4096]{1,0:T(8,128)(2,1)} %reduce-scatter.5.cloned.1.call-done) | copy-start | bytes 1769476
Sparse Core Ops, SparseCore 0:
  39.1 92.8 all-gather.2
  160.0 53.4 reduce-scatter.4
  215.8 53.2 reduce-scatter.2
